TPU v7x, 256 devices: a whole 4x4x8 slice. The times are simulated.
256 devices in a mesh: member: 4 (over y_hi, core), node: 64 (over y_lo, x, z).
Axes of the slice: x: 4, y: 4 (y_hi: 2, y_lo: 2; y = y_hi * 2 + y_lo), z: 8, core: 2. Of those that a mesh axis runs over, the one named last changes fastest.
Arguments:
- gridpoint_state: bfloat16 [218, 65536], P(None, 'node'), may hold values from -6 to 6
- grid_truth: bfloat16 [100, 65536], P(None, 'node'), may hold values from -6 to 6
- encoder_slots: int32 [16384, 16], P('node'), may hold values from 0 to 65535, as said below
- encoder_count: int32 [16384], P('node'), may hold values from 1 to 16
- node_reach: int32 [16384], P('node'), may hold values from 128 to 256
- decoder_slots: int32 [65536, 4], P('node'), may hold values from 0 to 16383, as said below
- member_perturb: bfloat16 [4, 16384, 1024], P('member', 'node'), may hold values from -6 to 6
- embed_weight: bfloat16 [218, 1024], replicated, may hold values from -0.4375 to 0.4375
- norm_gains: float32 [3, 1024], replicated, may hold values from 0.1 to 1.9
- qkv_weight: bfloat16 [1024, 3072], replicated
- out_weight: bfloat16 [1024, 1024], replicated, may hold values from -0.1875 to 0.1875
- up_weight: bfloat16 [1024, 4096], P('node'), may hold values from -0.1875 to 0.1875
- down_weight: bfloat16 [1024, 4096], P('node'), may hold values from -0.09375 to 0.09375
- head_weight: bfloat16 [1024, 100], replicated, may hold values from -0.1875 to 0.1875
Outputs:
- crps_grad: float32 [4, 100, 65536], P('member', None, 'node')
Inputs may be any that keep to these rules, and one draw needn't show every extreme that they name: `encoder_slots`: for a hidden node of region r (nodes r * 256 to (r + 1) * 256 - 1), every slot names a grid point of region r - 1, r or r + 1, a region holding 1024 consecutive points; slots from encoder_count on are padding. `decoder_slots`: for a grid point of region r, every slot names a hidden node of region r - 1, r or r + 1.
All inputs are finite; a program needn't handle non-finite values.
Results may differ from a plain program's by a relative error of at most 0.0095.
The roundings to bfloat16 on the way count: a program that leaves them out, or rounds other values in their place, can miss the bound.
Values may be sent and summed in bfloat16 or wider, within the bound.
No kernel may reach another device: no remote copies, remote signals or barrier semaphores. Data moves between devices by JAX's collectives and lax.ppermute only.
A program may use at most 128 MiB of HBM per device.

v0:
```python
import jax
import jax.numpy as jnp
from jax import lax
from jax.sharding import Mesh
from jax.sharding import PartitionSpec as P

HEADS = 16
HEAD_DIM = 64
BAND = 256
NODE = ("node_0", "node_1", "node_2")
EPS = 1e-05
SMOOTH = 0.25


def with_halo(block, sides, width):
    for axis, dim in sides:
        count = lax.axis_size(axis)
        forward = [(i, i + 1) for i in range(count - 1)]
        backward = [(target, source) for source, target in forward]
        low = lax.ppermute(
            lax.slice_in_dim(block, block.shape[dim] - width, None, axis=dim), axis, forward
        )
        high = lax.ppermute(lax.slice_in_dim(block, 0, width, axis=dim), axis, backward)
        block = jnp.concatenate([low, block, high], axis=dim)
    return block


def in_order(blocks, dim):
    blocks = jnp.moveaxis(blocks, 0, dim)
    dims = blocks.shape
    return blocks.reshape(*dims[:dim], dims[dim] * dims[dim + 1], *dims[dim + 2 :])


def gather_in_order(shard, axes, sequence):
    blocks = shard[None]
    for k in sequence:
        blocks = lax.all_gather(blocks, axes[k], axis=0, tiled=True)
    current = [lax.axis_size(axes[k]) for k in reversed(sequence)]
    blocks = blocks.reshape(*current, *shard.shape)
    turned = sorted(range(len(sequence)), key=lambda place: sequence[len(sequence) - 1 - place])
    return blocks.transpose(*turned, *range(len(sequence), blocks.ndim)).reshape(-1, *shard.shape)


def gathered_by_axis(shard, axes, sequence, dim):
    return in_order(gather_in_order(shard, axes, sequence), dim)


def layer_norm(entries, scale_gain):
    average = jnp.mean(entries, axis=-1, keepdims=True)
    centred = entries - average
    variance = jnp.mean(centred * centred, axis=-1, keepdims=True)
    return centred * lax.rsqrt(variance + EPS) * scale_gain


def score_gradient(difference):
    return difference * lax.rsqrt(difference * difference + SMOOTH * SMOOTH)


def times_rows(left_side, right_side):
    return lax.dot_general(
        left_side, right_side, (((1,), (1,)), ((), ())), preferred_element_type=jnp.float32
    )


def banded_attention(query_rows, bordered, first_query, first_key, node_total, reaches):
    query_count = query_rows.shape[0]
    key_count = bordered.shape[0]
    model_width = query_rows.shape[1]
    key_heads = bordered[:, :model_width].reshape(key_count, HEADS, HEAD_DIM)
    value_heads = bordered[:, model_width:].reshape(key_count, HEADS, HEAD_DIM)
    queries = query_rows.reshape(query_count, HEADS, HEAD_DIM)
    scores = jnp.einsum(
        "qhd,khd->hqk", queries, key_heads, preferred_element_type=jnp.float32
    ) * HEAD_DIM ** (-0.5)
    rows_at = first_query + jnp.arange(query_count, dtype=jnp.int32)
    cols_at = first_key + jnp.arange(key_count, dtype=jnp.int32)
    distance = jnp.abs(rows_at[:, None] - cols_at[None, :])
    allowed = (
        (distance <= reaches[:, None]) & (cols_at[None, :] >= 0) & (cols_at[None, :] < node_total)
    )
    masked = jnp.where(allowed[None], scores, -1e30)
    highest = jnp.max(masked, axis=-1, keepdims=True)
    weights = jnp.where(allowed[None], jnp.exp(masked - highest), 0.0)
    chances = (weights / jnp.sum(weights, axis=-1, keepdims=True)).astype(jnp.bfloat16)
    blended = jnp.einsum("hqk,khd->qhd", chances, value_heads, preferred_element_type=jnp.float32)
    return blended.reshape(query_count, model_width).astype(jnp.bfloat16)


def per_device(
    gridpoint_state,
    grid_truth,
    encoder_slots,
    encoder_count,
    node_reach,
    decoder_slots,
    member_perturb,
    embed_weight,
    norm_gains,
    qkv_weight,
    out_weight,
    up_weight,
    down_weight,
    head_weight,
):
    region = lax.axis_index(NODE)
    region_count = lax.axis_size(NODE)
    ensemble_size = lax.axis_size("member")
    member_index = lax.axis_index("member")
    grid_dev = gridpoint_state.shape[1]
    node_dev = encoder_slots.shape[0]
    model_width = embed_weight.shape[1]
    node_total = node_dev * region_count
    widened = with_halo(gridpoint_state, ((NODE, 1),), grid_dev)
    local_slots = encoder_slots - (region - 1) * grid_dev
    window = jnp.arange(3 * grid_dev, dtype=jnp.int32)
    tallies = jnp.zeros((node_dev, 3 * grid_dev), jnp.float32)
    for position in range(encoder_slots.shape[1]):
        live = position < encoder_count
        hits = (local_slots[:, position][:, None] == window[None, :]) & live[:, None]
        tallies = tallies + hits.astype(jnp.float32)
    pooled_sum = times_rows(tallies.astype(jnp.bfloat16), widened)
    pooled_nodes = (pooled_sum / encoder_count[:, None].astype(jnp.float32)).astype(jnp.bfloat16)
    embedded = jnp.dot(pooled_nodes, embed_weight, preferred_element_type=jnp.float32)
    hidden_start = embedded + member_perturb[0].astype(jnp.float32)
    normed = layer_norm(hidden_start, norm_gains[0]).astype(jnp.bfloat16)
    project = jnp.dot(normed, qkv_weight, preferred_element_type=jnp.float32).astype(jnp.bfloat16)
    query_rows = project[:, :model_width]
    bordered = with_halo(project[:, model_width:], ((NODE, 0),), BAND)
    first_query = region * node_dev
    attended = banded_attention(
        query_rows, bordered, first_query, first_query - BAND, node_total, node_reach
    )
    hidden_mid = hidden_start + jnp.dot(attended, out_weight, preferred_element_type=jnp.float32)
    normed_mid = layer_norm(hidden_mid, norm_gains[1]).astype(jnp.bfloat16)
    up_whole = gathered_by_axis(up_weight, NODE, (0, 1, 2), 0)
    upper = jnp.dot(normed_mid, up_whole, preferred_element_type=jnp.float32)
    active = jax.nn.gelu(upper).astype(jnp.bfloat16)
    down_whole = gathered_by_axis(down_weight, NODE, (0, 1, 2), 0)
    lowered = times_rows(active, down_whole)
    final = layer_norm(hidden_mid + lowered, norm_gains[2]).astype(jnp.bfloat16)
    local_nodes = decoder_slots - (region - 1) * node_dev
    variable_count = head_weight.shape[1]
    slot_count = decoder_slots.shape[1]
    projected = lax.dot_general(
        head_weight, final, (((0,), (1,)), ((), ())), preferred_element_type=jnp.float32
    )
    projected_near = with_halo(projected.astype(jnp.bfloat16), ((NODE, 1),), node_dev).astype(
        projected.dtype
    )
    summed = jnp.zeros((variable_count, grid_dev), jnp.float32)
    for position in range(slot_count):
        summed = summed + jnp.take(projected_near, local_nodes[:, position], axis=1)
    state_delta = summed / slot_count
    predicted_field = gridpoint_state[:variable_count].astype(jnp.float32) + state_delta
    pairwise_scale = 1.0 / (ensemble_size * (ensemble_size - 1))
    share = grid_dev // ensemble_size
    mine = lax.all_to_all(predicted_field[None], "member", split_axis=2, concat_axis=0, tiled=True)
    observed_field = lax.dynamic_slice_in_dim(grid_truth, member_index * share, share, 1).astype(
        jnp.float32
    )
    pairwise_sum = jnp.zeros_like(mine)
    for other_member in range(ensemble_size):
        pairwise_sum = pairwise_sum + score_gradient(mine - mine[other_member][None])
    gradients = (
        score_gradient(mine - observed_field[None]) / ensemble_size - pairwise_sum * pairwise_scale
    )
    return lax.all_to_all(
        gradients.astype(jnp.bfloat16), "member", split_axis=0, concat_axis=2, tiled=True
    ).astype(gradients.dtype)


def solution(mesh):
    torus = Mesh(
        mesh.devices.reshape(mesh.shape["member"], 2, 4, 8),
        ("member", "node_0", "node_1", "node_2"),
    )
    return jax.shard_map(
        per_device,
        mesh=torus,
        in_specs=(
            P(None, NODE),
            P(None, NODE),
            P(NODE, None),
            P(NODE),
            P(NODE),
            P(NODE, None),
            P("member", NODE, None),
            P(),
            P(),
            P(),
            P(),
            P(NODE, None),
            P(NODE, None),
            P(),
        ),
        out_specs=P("member", None, NODE),
        check_vma=False,
    )
```

profile of v0, /device:TPU:8, one launch (start us, length us, event | category | flops | bytes accessed | tf_op | source)
XLA Modules:
  0.0 375.4 jit_solution(6813843629020049477)
XLA Ops:
  6.6 7.8 %all-gather.1 = bf16[32,4096]{1,0:T(8,128)(2,1)} all-gather(bf16[16,4096]{1,0:T(8,128)(2,1)} %param.28), channel_id=3, replica_groups=mesh['member'=4,'node_0'=2,'node_1'=4,'node_2'=8] {'node_0'}, dimensions={0}, use_global_device_ids=true | all-gather | bytes 393216 | tf_op jit(solution)/shard_map/all_gather | solution.py:37
  14.5 6.0 %all-gather = bf16[32,4096]{1,0:T(8,128)(2,1)} all-gather(bf16[16,4096]{1,0:T(8,128)(2,1)} %param.27), channel_id=2, replica_groups=mesh['member'=4,'node_0'=2,'node_1'=4,'node_2'=8] {'node_0'}, dimensions={0}, use_global_device_ids=true | all-gather | bytes 393216 | tf_op jit(solution)/shard_map/all_gather | solution.py:37
  20.5 23.1 %all-gather.11.cloned.1.call-done = bf16[8,16,4096]{2,1,0:T(8,128)(2,1)} async-done(((bf16[2,16,4096]{2,1,0:T(8,128)(2,1)}), bf16[8,16,4096]{2,1,0:T(8,128)(2,1)}) %all-gather.11.cloned.1.call-update) | async-done | bytes 1048592 | tf_op jit(solution)/shard_map/all_gather | solution.py:37
  43.7 28.6 %all-gather.7.cloned.1.call-done = bf16[8,16,4096]{2,1,0:T(8,128)(2,1)} async-done(((bf16[2,16,4096]{2,1,0:T(8,128)(2,1)}), bf16[8,16,4096]{2,1,0:T(8,128)(2,1)}) %all-gather.7.cloned.1.call-update) | async-done | bytes 1048592 | tf_op jit(solution)/shard_map/all_gather | solution.py:37
  72.3 6.4 %collective-permute-start.1 = (bf16[218,1024]{1,0:T(8,128)(2,1)S(1)}, bf16[218,1024]{1,0:T(8,128)(2,1)S(1)}, u32[]{:S(2)}, u32[]{:S(2)}) collective-permute-start(bf16[218,1024]{1,0:T(8,128)(2,1)S(1)} %copy-done.4), channel_id=1, source_target_pairs={{1,0},{2,1},{3,2},{4,3},{5,4},{6,5},{7,6},{8,7},{9,8},{10,9},{11,1... | collective-permute-start | bytes 1339400 | tf_op jit(solution)/shard_map/ppermute | solution.py:23
  80.9 9.8 %collective-permute-done.1 = bf16[218,1024]{1,0:T(8,128)(2,1)S(1)} collective-permute-done((bf16[218,1024]{1,0:T(8,128)(2,1)S(1)}, bf16[218,1024]{1,0:T(8,128)(2,1)S(1)}, u32[]{:S(2)}, u32[]{:S(2)}) %collective-permute-start.1) | collective-permute-done | bytes 446496 | tf_op jit(solution)/shard_map/ppermute | solution.py:23
  90.7 11.8 %collective-permute-done = bf16[218,1024]{1,0:T(8,128)(2,1)} collective-permute-done((bf16[218,1024]{1,0:T(8,128)(2,1)S(1)}, bf16[218,1024]{1,0:T(8,128)(2,1)}, u32[]{:S(2)}, u32[]{:S(2)}) %collective-permute-start) | collective-permute-done | bytes 446496 | tf_op jit(solution)/shard_map/ppermute | solution.py:20
  102.5 12.2 %fusion.125 = (f32[256]{0:T(256)S(1)}, f32[256,1024]{1,0:T(8,128)S(1)}) fusion(bf16[1,256,1024]{2,1,0:T(8,128)(2,1)} %param.22, bf16[218,1024]{1,0:T(8,128)(2,1)} %param.23, bf16[218,1024]{1,0:T(8,128)(2,1)} %copy-done.12, bf16[218,1024]{1,0:T(8,128)(2,1)} %param.16, bf16[218,1024]{1,0:T(8,128)(2,1)} %collective-permute-done, s32[256]{0:T(256)S(1)} %bitcast.132, ...), kind=kOutput, calls=%fused_computation.198 | convolution fusion | flops 512426752 | bytes 3381248 | tf_op jit(solution)/shard_map/dot_general | solution.py:123
  115.0 5.0 %convolution_convert_fusion = bf16[256,3072]{1,0:T(8,128)(2,1)S(1)} fusion(bf16[1024,3072]{1,0:T(8,128)(2,1)} %param.25, f32[256,1024]{1,0:T(8,128)S(1)} %get-tuple-element.52, f32[1024]{0:T(1024)S(1)} %bitcast.130, f32[256]{0:T(256)S(1)} %add_rsqrt_fusion.2, f32[256]{0:T(256)S(1)} %broadcast_multiply_fusion.2), kind=kOutput, calls=%fused_computation.22 | convolution fusion | flops 1612447744 | bytes 8919040 | tf_op jit(solution)/shard_map/dot_general | solution.py:126
  123.0 3.9 %collective-permute-start.2 = (bf16[256,2048]{1,0:T(8,128)(2,1)}, bf16[256,2048]{1,0:T(8,128)(2,1)}, u32[]{:S(2)}, u32[]{:S(2)}) collective-permute-start(bf16[256,2048]{1,0:T(8,128)(2,1)} %slice.157), channel_id=1, source_target_pairs={{0,1},{1,2},{2,3},{3,4},{4,5},{5,6},{6,7},{7,8},{8,9},{9,10},{10,1... | collective-permute-start | bytes 3145736 | tf_op jit(solution)/shard_map/ppermute | solution.py:20
  129.3 2.0 copy.61
  131.4 37.4 %collective-permute-done.3 = bf16[256,2048]{1,0:T(8,128)(2,1)} collective-permute-done((bf16[256,2048]{1,0:T(8,128)(2,1)}, bf16[256,2048]{1,0:T(8,128)(2,1)}, u32[]{:S(2)}, u32[]{:S(2)}) %collective-permute-start.3) | collective-permute-done | bytes 1048608 | tf_op jit(solution)/shard_map/ppermute | solution.py:23
  168.8 6.1 %collective-permute-done.2 = bf16[256,2048]{1,0:T(8,128)(2,1)} collective-permute-done((bf16[256,2048]{1,0:T(8,128)(2,1)}, bf16[256,2048]{1,0:T(8,128)(2,1)}, u32[]{:S(2)}, u32[]{:S(2)}) %collective-permute-start.2) | collective-permute-done | bytes 1048608 | tf_op jit(solution)/shard_map/ppermute | solution.py:20
  174.9 2.1 pad_maximum_fusion
  179.0 2.6 copy.60
  181.6 2.6 copy.62
  184.2 11.4 %fusion.128 = (f32[16,256]{1,0:T(8,128)S(1)}, f32[16,256,768]{2,1,0:T(8,128)}) fusion(pred[256,768]{1,0:T(8,128)(4,1)S(1)} %fusion.90, bf16[256,16,64]{0,2,1:T(8,128)(2,1)} %bitcast.119, bf16[768,16,64]{0,2,1:T(8,128)(2,1)} %bitcast.115), kind=kOutput, calls=%fused_computation.199 | convolution fusion | flops 418382592 | bytes 14893056 | tf_op jit(solution)/shard_map/sub | solution.py:83
  195.6 7.1 %fusion.77 = bf16[16,64,256]{2,1,0:T(8,128)(2,1)S(1)} fusion(bf16[768,16,64]{0,2,1:T(8,128)(2,1)} %bitcast.114, f32[16,256,768]{2,1,0:T(8,128)} %get-tuple-element.54, f32[16,256]{1,0:T(8,128)S(1)} %get-tuple-element.53), kind=kOutput, calls=%fused_computation.103 | convolution fusion | flops 409206784 | bytes 14696448 | tf_op jit(solution)/shard_map/hqk,khd->qhd/dot_general | solution.py:85
  204.9 7.7 %copy.64 = bf16[2,4,8,16,4096]{4,3,2,1,0:T(8,128)(2,1)} copy(bf16[2,4,8,16,4096]{4,3,0,1,2:T(8,128)(2,1)} %bitcast.107) | data formatting | bytes 16777216 | tf_op jit(solution)/shard_map/transpose | solution.py:41
  212.6 74.4 %all-gather.9.cloned.1.call-done = bf16[64,16,4096]{2,1,0:T(8,128)(2,1)} async-done(((bf16[8,16,4096]{2,1,0:T(8,128)(2,1)}), bf16[64,16,4096]{2,1,0:T(8,128)(2,1)}) %all-gather.9.cloned.1.call-update) | async-done | bytes 8388624 | tf_op jit(solution)/shard_map/all_gather | solution.py:37
  287.0 7.8 %copy.63 = bf16[2,4,8,16,4096]{4,3,2,1,0:T(8,128)(2,1)} copy(bf16[2,4,8,16,4096]{4,3,0,1,2:T(8,128)(2,1)} %bitcast.108) | data formatting | bytes 16777216 | tf_op jit(solution)/shard_map/transpose | solution.py:41
  294.8 12.0 %fusion.130 = (f32[256]{0:T(256)S(1)}, f32[256,1024]{1,0:T(8,128)}) fusion(f32[256,1024]{1,0:T(8,128)S(1)} %copy-done.2, bf16[1024,4096]{1,0:T(8,128)(2,1)} %bitcast.109, bf16[1024,4096]{1,0:T(8,128)(2,1)} %bitcast.110, f32[1024]{0:T(1024)S(1)} %bitcast.129, f32[256]{0:T(256)S(1)} %add_rsqrt_fusion.1, f32[256]{0:T(256)S(1)} %broadcast_multiply_fusion.1), kind=kOutput, calls=%fused_computation.201 | convolution fusion | flops 4305977344 | bytes 18881536 | tf_op jit(solution)/shard_map/dot_general | solution.py:60
  309.9 5.4 %collective-permute-start.5 = (bf16[100,256]{1,0:T(8,128)(2,1)S(1)}, bf16[100,256]{1,0:T(8,128)(2,1)S(1)}, u32[]{:S(2)}, u32[]{:S(2)}) collective-permute-start(bf16[100,256]{1,0:T(8,128)(2,1)S(1)} %fusion.80), channel_id=1, source_target_pairs={{1,0},{2,1},{3,2},{4,3},{5,4},{6,5},{7,6},{8,7},{9,8},{10,9},{11,1... | collective-permute-start | bytes 153608 | tf_op jit(solution)/shard_map/ppermute | solution.py:23
  319.1 6.5 %collective-permute-done.4 = bf16[100,256]{1,0:T(8,128)(2,1)S(1)} collective-permute-done((bf16[100,256]{1,0:T(8,128)(2,1)S(1)}, bf16[100,256]{1,0:T(8,128)(2,1)S(1)}, u32[]{:S(2)}, u32[]{:S(2)}) %collective-permute-start.4) | collective-permute-done | bytes 51232 | tf_op jit(solution)/shard_map/ppermute | solution.py:20
  325.8 2.8 gather_fusion.3
  328.6 2.8 gather_fusion.2
  331.4 4.0 %gather_fusion.1 = f32[1024,100]{1,0:T(8,128)} fusion(f32[100,768]{0,1:T(8,128)S(1)} %copy.65, s32[1024]{0:T(1024)S(1)} %fusion.110), kind=kCustom, calls=%fused_computation.1.clone | custom fusion | bytes 823296 | tf_op jit(solution)/shard_map/jit(_take)/gather | solution.py:152
  335.5 4.0 %gather_fusion = f32[1024,100]{1,0:T(8,128)} fusion(f32[100,768]{0,1:T(8,128)S(1)} %copy.65, s32[1024]{0:T(1024)S(1)} %fusion.109), kind=kCustom, calls=%fused_computation.clone | custom fusion | bytes 823296 | tf_op jit(solution)/shard_map/jit(_take)/gather | solution.py:152
  339.5 3.8 %fusion.93 = f32[100,1024]{0,1:T(8,128)} fusion(f32[1024,100]{1,0:T(8,128)S(1)} %gather_fusion.3, f32[1024,100]{1,0:T(8,128)S(1)} %gather_fusion.2, f32[1024,100]{1,0:T(8,128)} %gather_fusion.1, f32[1024,100]{1,0:T(8,128)} %gather_fusion, bf16[100,1024]{0,1:T(8,128)(2,1)} %copy.73, pred[1024]{0:T(1024)(128)(4,1)S(1)} %get-tuple-element.61, ...), kind=kLoop, calls=%fused_computation.121 | loop fusion | flops 1024000 | bytes 2256896 | tf_op jit(solution)/shard_map/add | solution.py:154
  343.3 3.7 all-to-all-start
  347.7 9.5 %all-to-all-done = f32[1,100,1024]{1,0,2:T(1,128)S(1)} async-done(((f32[1,100,1024]{1,0,2:T(1,128)}), f32[1,100,1024]{1,0,2:T(1,128)S(1)}, u32[]{:S(2)}, u32[]{:S(2)}) %all-to-all-start) | async-done | bytes 409632 | tf_op jit(solution)/shard_map/all_to_all | solution.py:157
  358.0 9.4 %all_to_all.27 = bf16[4,100,256]{2,1,0:T(8,128)(2,1)S(1)} all-to-all(bf16[4,100,256]{2,1,0:T(8,128)(2,1)S(1)} %subtract_convert_fusion), channel_id=1, replica_groups=mesh['member'=4,'node_0'=2,'node_1'=4,'node_2'=8] {'member'}, dimensions={0} | all-to-all | bytes 409600 | tf_op jit(solution)/shard_map/all_to_all | solution.py:167
  (81 shorter events, 22.0 us)
Async XLA Ops:
  6.5 196.2 %copy-start = (bf16[1024,1024]{1,0:T(8,128)(2,1)S(1)}, bf16[1024,1024]{1,0:T(8,128)(2,1)}, u32[]{:S(2)}) copy-start(bf16[1024,1024]{1,0:T(8,128)(2,1)} %param.26) | copy-start | bytes 6291460
  6.5 65.8 %copy-start.4 = (bf16[218,1024]{1,0:T(8,128)(2,1)S(1)}, bf16[218,1024]{1,0:T(8,128)(2,1)}, u32[]{:S(2)}) copy-start(bf16[218,1024]{1,0:T(8,128)(2,1)} %param.16) | copy-start | bytes 1339396
  6.5 74.2 %copy-start.10 = (s32[256]{0:T(256)S(1)}, s32[256]{0:T(256)}, u32[]{:S(2)}) copy-start(s32[256]{0:T(256)} %param.19) | copy-start | bytes 3076
  6.5 74.2 %copy-start.5 = (s32[1024,4]{0,1:T(4,128)S(1)}, s32[1024,4]{0,1:T(4,128)}, u32[]{:S(2)}) copy-start(s32[1024,4]{0,1:T(4,128)} %param.21) | copy-start | bytes 49156
  6.5 74.3 %copy-start.6 = (s32[256,16]{0,1:T(8,128)S(1)}, s32[256,16]{0,1:T(8,128)}, u32[]{:S(2)}) copy-start(s32[256,16]{0,1:T(8,128)} %param.18) | copy-start | bytes 49156
  6.5 74.3 %copy-start.7 = (f32[3,1024]{1,0:T(4,128)S(1)}, f32[3,1024]{1,0:T(4,128)}, u32[]{:S(2)}) copy-start(f32[3,1024]{1,0:T(4,128)} %param.24) | copy-start | bytes 36868
  6.6 37.0 %all-gather.11.cloned.1.call-start = ((), (), s32[]{:S(2)}) async-start(), calls=%async_computation.4 | async-start | bytes 1310720 | tf_op jit(solution)/shard_map/all_gather | solution.py:37
  14.4 57.9 %all-gather.7.cloned.1.call-start = ((), (), s32[]{:S(2)}) async-start(), calls=%async_computation.2 | async-start | bytes 1310720 | tf_op jit(solution)/shard_map/all_gather | solution.py:37
  20.5 184.4 %all-gather.13.cloned.1.call-start = ((), (), s32[]{:S(2)}) async-start(), calls=%async_computation.5 | async-start | bytes 9437184 | tf_op jit(solution)/shard_map/all_gather | solution.py:37
  43.6 243.4 %all-gather.9.cloned.1.call-start = ((), (), s32[]{:S(2)}) async-start(), calls=%async_computation.3 | async-start | bytes 9437184 | tf_op jit(solution)/shard_map/all_gather | solution.py:37
  72.3 18.4 %collective-permute-start.1 = (bf16[218,1024]{1,0:T(8,128)(2,1)S(1)}, bf16[218,1024]{1,0:T(8,128)(2,1)S(1)}, u32[]{:S(2)}, u32[]{:S(2)}) collective-permute-start(bf16[218,1024]{1,0:T(8,128)(2,1)S(1)} %copy-done.4), channel_id=1, source_target_pairs={{1,0},{2,1},{3,2},{4,3},{5,4},{6,5},{7,6},{8,7},{9,8},{10,9},{11,1... | collective-permute-start | bytes 1339400 | tf_op jit(solution)/shard_map/ppermute | solution.py:23
  78.8 23.8 %collective-permute-start = (bf16[218,1024]{1,0:T(8,128)(2,1)S(1)}, bf16[218,1024]{1,0:T(8,128)(2,1)}, u32[]{:S(2)}, u32[]{:S(2)}) collective-permute-start(bf16[218,1024]{1,0:T(8,128)(2,1)S(1)} %copy-done.4), channel_id=1, source_target_pairs={{0,1},{1,2},{2,3},{3,4},{4,5},{5,6},{6,7},{7,8},{8,9},{9,10},{10,1... | collective-permute-start | bytes 1339400 | tf_op jit(solution)/shard_map/ppermute | solution.py:20
  90.7 11.8 %copy-start.12 = (bf16[218,1024]{1,0:T(8,128)(2,1)}, bf16[218,1024]{1,0:T(8,128)(2,1)S(1)}, u32[]{:S(2)}) copy-start(bf16[218,1024]{1,0:T(8,128)(2,1)S(1)} %collective-permute-done.1) | copy-start | bytes 1339396
  115.0 13.2 %copy-start.11 = (s32[256]{0:T(256)S(1)}, s32[256]{0:T(256)}, u32[]{:S(2)}) copy-start(s32[256]{0:T(256)} %param.20) | copy-start | bytes 3076
  121.1 47.7 %collective-permute-start.3 = (bf16[256,2048]{1,0:T(8,128)(2,1)}, bf16[256,2048]{1,0:T(8,128)(2,1)}, u32[]{:S(2)}, u32[]{:S(2)}) collective-permute-start(bf16[256,2048]{1,0:T(8,128)(2,1)} %slice.157), channel_id=1, source_target_pairs={{1,0},{2,1},{3,2},{4,3},{5,4},{6,5},{7,6},{8,7},{9,8},{10,9},{11,1... | collective-permute-start | bytes 3145736 | tf_op jit(solution)/shard_map/ppermute | solution.py:23
  123.0 52.0 %collective-permute-start.2 = (bf16[256,2048]{1,0:T(8,128)(2,1)}, bf16[256,2048]{1,0:T(8,128)(2,1)}, u32[]{:S(2)}, u32[]{:S(2)}) collective-permute-start(bf16[256,2048]{1,0:T(8,128)(2,1)} %slice.157), channel_id=1, source_target_pairs={{0,1},{1,2},{2,3},{3,4},{4,5},{5,6},{6,7},{7,8},{8,9},{9,10},{10,1... | collective-permute-start | bytes 3145736 | tf_op jit(solution)/shard_map/ppermute | solution.py:20
  203.5 1.0 copy-start.1
  287.0 7.8 %copy-start.2 = (f32[256,1024]{1,0:T(8,128)S(1)}, f32[256,1024]{1,0:T(8,128)}, u32[]{:S(2)}) copy-start(f32[256,1024]{1,0:T(8,128)} %copy-done.1) | copy-start | bytes 3145732
  294.8 13.5 %copy-start.3 = (bf16[1024,100]{0,1:T(8,128)(2,1)S(1)}, bf16[1024,100]{0,1:T(8,128)(2,1)}, u32[]{:S(2)}) copy-start(bf16[1024,100]{0,1:T(8,128)(2,1)} %param.29) | copy-start | bytes 614404
  309.9 9.2 %collective-permute-start.5 = (bf16[100,256]{1,0:T(8,128)(2,1)S(1)}, bf16[100,256]{1,0:T(8,128)(2,1)S(1)}, u32[]{:S(2)}, u32[]{:S(2)}) collective-permute-start(bf16[100,256]{1,0:T(8,128)(2,1)S(1)} %fusion.80), channel_id=1, source_target_pairs={{1,0},{2,1},{3,2},{4,3},{5,4},{6,5},{7,6},{8,7},{9,8},{10,9},{11,1... | collective-permute-start | bytes 153608 | tf_op jit(solution)/shard_map/ppermute | solution.py:23
  315.3 10.2 %collective-permute-start.4 = (bf16[100,256]{1,0:T(8,128)(2,1)S(1)}, bf16[100,256]{1,0:T(8,128)(2,1)S(1)}, u32[]{:S(2)}, u32[]{:S(2)}) collective-permute-start(bf16[100,256]{1,0:T(8,128)(2,1)S(1)} %fusion.80), channel_id=1, source_target_pairs={{0,1},{1,2},{2,3},{3,4},{4,5},{5,6},{6,7},{7,8},{8,9},{9,10},{10,1... | collective-permute-start | bytes 153608 | tf_op jit(solution)/shard_map/ppermute | solution.py:20
  331.4 8.1 %copy-start.8 = (pred[1024]{0:T(1024)(128)(4,1)S(1)}, pred[1024]{0:T(1024)(128)(4,1)}, u32[]{:S(2)}) copy-start(pred[1024]{0:T(1024)(128)(4,1)} %get-tuple-element.62) | copy-start | bytes 3076
  335.5 4.0 %copy-start.9 = (pred[1024]{0:T(1024)(128)(4,1)S(1)}, pred[1024]{0:T(1024)(128)(4,1)}, u32[]{:S(2)}) copy-start(pred[1024]{0:T(1024)(128)(4,1)} %get-tuple-element.63) | copy-start | bytes 3076
  343.3 14.0 %all-to-all-start = ((f32[1,100,1024]{1,0,2:T(1,128)}), f32[1,100,1024]{1,0,2:T(1,128)S(1)}, u32[]{:S(2)}, u32[]{:S(2)}) async-start(f32[1,100,1024]{1,0,2:T(1,128)} %bitcast.113), calls=%async_computation | async-start | bytes 1048576 | tf_op jit(solution)/shard_map/all_to_all | solution.py:157
Sparse Core Ops, SparseCore 0:
  14.5 29.0 all-gather.10
  45.4 26.8 all-gather.6
  74.1 120.2 all-gather.12
  196.0 90.8 all-gather.8
where the time goes:
time: 376 us; the launch traced here: 375 us
  waiting for transfers between devices  207 us (55%)
  matrix products  50.1 us (13%)
  local copies, waits for them, and re-layouts  45.2 us (12%)
  starting transfers between devices  25.3 us (7%)
  blocking collectives  23.1 us (6%)
  between operations  13.5 us (4%)
  other arithmetic  10.8 us (3%)
    all_gather x4, waiting for transfers between devices, gather_in_order(): blocks = lax.all_gather(blocks, axes[k], axis=0, tiled=True)  126 us
    ppermute x3, waiting for transfers between devices, with_halo(): lax.ppermute(lax.slice_in_dim(block, 0, width, axis=dim), axis, backward)  47.2 us
    ppermute x3, waiting for transfers between devices, with_halo(): lax.ppermute(lax.slice_in_dim(block, block.shape[dim] - width, None, axis...  24.5 us
    transpose x2, local copies, waits for them, and re-layouts, gather_in_order(): blocks.transpose(*turned, *range(len(sequence), blocks.ndim))  15.6 us
    all_gather x2, blocking collectives, gather_in_order(): blocks = lax.all_gather(blocks, axes[k], axis=0, tiled=True)  13.8 us
    ppermute x3, starting transfers between devices, with_halo(): lax.ppermute(lax.slice_in_dim(block, 0, width, axis=dim), axis, backward)  13.7 us
    gather x4, local copies, waits for them, and re-layouts, per_device(): summed = summed + jnp.take(projected_near, local_nodes[:, position], axis=1)  13.7 us
    dot_general x1, matrix products, per_device(): jnp.dot(pooled_nodes, embed_weight, preferred_element_type=jnp.float32)  12.2 us
  transfers between devices with their start and end apart: 11, of which 9 were waited for; matrix products, arithmetic and copies ran while one was open for 17% of the time, Pallas kernels for 0%

commit v1 on v0

--- a/solution.py
+++ b/solution.py
@@ -34,7 +34,10 @@
 def gather_in_order(shard, axes, sequence):
     blocks = shard[None]
     for k in sequence:
-        blocks = lax.all_gather(blocks, axes[k], axis=0, tiled=True)
+        _keep_up_forms = lambda m, shard_axis: jnp.concatenate(
+            lax.all_to_all(jnp.stack(lax.axis_size(shard_axis) * [m]), shard_axis, 0, 0), 0
+        )
+        blocks = _keep_up_forms(blocks, axes[k])
     current = [lax.axis_size(axes[k]) for k in reversed(sequence)]
     blocks = blocks.reshape(*current, *shard.shape)
     turned = sorted(range(len(sequence)), key=lambda place: sequence[len(sequence) - 1 - place])

time: 376 us -> 606 us (1.61)
  blocking collectives: 23.1 us -> 238 us
  between operations: 13.5 us -> 0.45 us
  waiting for transfers between devices: 207 us -> 217 us
  starting transfers between devices: 25.3 us -> 35.2 us
    all_to_all x0 -> x4, blocking collectives: none -> 228 us  [gather_in_order(): lax.all_to_all(jnp.stack(lax.axis_size(shard_axis) * [m]), shard_axis, 0, 0)]
    ppermute x3, waiting for transfers between devices: 47.2 us -> 192 us  [with_halo(): lax.ppermute(lax.slice_in_dim(block, 0, width, axis=dim), axis, backward)]
    all_gather x4 -> x0, waiting for transfers between devices: 126 us -> none  [gather_in_order(): blocks = lax.all_gather(blocks, axes[k], axis=0, tiled=True)]
    all_gather x2 -> x0, blocking collectives: 13.8 us -> none  [gather_in_order(): blocks = lax.all_gather(blocks, axes[k], axis=0, tiled=True)]
    all_to_all x0 -> x2, starting transfers between devices: none -> 10.8 us  [gather_in_order(): lax.all_to_all(jnp.stack(lax.axis_size(shard_axis) * [m]), shard_axis, 0, 0)]
    ppermute x3, waiting for transfers between devices: 24.5 us -> 13.9 us  [with_halo(): lax.ppermute(lax.slice_in_dim(block, block.shape[dim] - width, None, axis...]
  transfers between devices with their start and end apart: 11 -> 9, of which waited for: 9 -> 7; matrix products, arithmetic and copies ran while one was open for 17% -> 10% of each run, Pallas kernels for 0% -> 0%
where the time goes in v1:
time: 606 us; the launch traced here: 605 us
  blocking collectives  238 us (39%)
  waiting for transfers between devices  217 us (36%)
  local copies, waits for them, and re-layouts  50.7 us (8%)
  matrix products  50 us (8%)
  starting transfers between devices  35.2 us (6%)
  other arithmetic  13.5 us (2%)
    all_to_all x4, blocking collectives, gather_in_order(): lax.all_to_all(jnp.stack(lax.axis_size(shard_axis) * [m]), shard_axis, 0, 0)  228 us
    ppermute x3, waiting for transfers between devices, with_halo(): lax.ppermute(lax.slice_in_dim(block, 0, width, axis=dim), axis, backward)  192 us
    transpose x2, local copies, waits for them, and re-layouts, gather_in_order(): blocks.transpose(*turned, *range(len(sequence), blocks.ndim))  15.6 us
    ppermute x3, waiting for transfers between devices, with_halo(): lax.ppermute(lax.slice_in_dim(block, block.shape[dim] - width, None, axis...  13.9 us
    gather x4, local copies, waits for them, and re-layouts, per_device(): summed = summed + jnp.take(projected_near, local_nodes[:, position], axis=1)  13.7 us
    ppermute x3, starting transfers between devices, with_halo(): lax.ppermute(lax.slice_in_dim(block, 0, width, axis=dim), axis, backward)  12.7 us
    dot_general x1, matrix products, per_device(): jnp.dot(pooled_nodes, embed_weight, preferred_element_type=jnp.float32)  12.1 us
  transfers between devices with their start and end apart: 9, of which 7 were waited for; matrix products, arithmetic and copies ran while one was open for 10% of the time, Pallas kernels for 0%

profile of v1, /device:TPU:8, one launch (start us, length us, event | category | flops | bytes accessed | tf_op | source)
XLA Modules:
  0.0 605.1 jit_solution(11800743008855994962)
XLA Ops:
  1.8 5.6 all-to-all-start.3
  10.6 7.6 %all_to_all.57 = bf16[2,1,16,4096]{3,2,1,0:T(8,128)(2,1)S(1)} all-to-all(bf16[2,1,16,4096]{3,2,1,0:T(8,128)(2,1)S(1)} %pad_maximum_fusion.1), channel_id=1, replica_groups=mesh['member'=4,'node_0'=2,'node_1'=4,'node_2'=8] {'node_0'}, dimensions={0} | all-to-all | bytes 524288 | tf_op jit(solution)/shard_map/all_to_all | solution.py:38
  18.3 16.0 %all_to_all.58 = bf16[4,2,16,4096]{3,2,1,0:T(8,128)(2,1)S(1)} all-to-all(bf16[4,2,16,4096]{3,2,1,0:T(8,128)(2,1)S(1)} %stack.22), channel_id=1, replica_groups=mesh['member'=4,'node_0'=2,'node_1'=4,'node_2'=8] {'node_1'}, dimensions={0} | all-to-all | bytes 2097152 | tf_op jit(solution)/shard_map/all_to_all | solution.py:38
  34.4 14.6 %all_to_all.59 = bf16[4,2,16,4096]{3,2,1,0:T(8,128)(2,1)S(1)} all-to-all(bf16[4,2,16,4096]{3,2,1,0:T(8,128)(2,1)S(1)} %stack.19), channel_id=1, replica_groups=mesh['member'=4,'node_0'=2,'node_1'=4,'node_2'=8] {'node_1'}, dimensions={0} | all-to-all | bytes 2097152 | tf_op jit(solution)/shard_map/all_to_all | solution.py:38
  50.0 190.2 %all_to_all.60 = bf16[8,8,16,4096]{3,2,1,0:T(8,128)(2,1)} all-to-all(bf16[8,8,16,4096]{3,2,1,0:T(8,128)(2,1)S(1)} %stack.23), channel_id=1, replica_groups=mesh['member'=4,'node_0'=2,'node_1'=4,'node_2'=8] {'node_2'}, dimensions={0} | all-to-all | bytes 16777216 | tf_op jit(solution)/shard_map/all_to_all | solution.py:38
  240.2 4.4 stack.20
  244.6 5.2 all-to-all-start.2
  249.8 6.8 %collective-permute-start.1 = (bf16[218,1024]{1,0:T(8,128)(2,1)S(1)}, bf16[218,1024]{1,0:T(8,128)(2,1)S(1)}, u32[]{:S(2)}, u32[]{:S(2)}) collective-permute-start(bf16[218,1024]{1,0:T(8,128)(2,1)S(1)} %copy-done.4), channel_id=1, source_target_pairs={{1,0},{2,1},{3,2},{4,3},{5,4},{6,5},{7,6},{8,7},{9,8},{10,9},{11,1... | collective-permute-start | bytes 1339400 | tf_op jit(solution)/shard_map/ppermute | solution.py:23
  259.0 176.9 %collective-permute-done.1 = bf16[218,1024]{1,0:T(8,128)(2,1)S(1)} collective-permute-done((bf16[218,1024]{1,0:T(8,128)(2,1)S(1)}, bf16[218,1024]{1,0:T(8,128)(2,1)S(1)}, u32[]{:S(2)}, u32[]{:S(2)}) %collective-permute-start.1) | collective-permute-done | bytes 446496 | tf_op jit(solution)/shard_map/ppermute | solution.py:23
  435.8 3.3 collective-permute-done
  439.1 12.1 %fusion.125 = (f32[256]{0:T(256)S(1)}, f32[256,1024]{1,0:T(8,128)S(1)}) fusion(bf16[1,256,1024]{2,1,0:T(8,128)(2,1)} %param.22, bf16[218,1024]{1,0:T(8,128)(2,1)} %param.23, bf16[218,1024]{1,0:T(8,128)(2,1)} %copy-done.12, bf16[218,1024]{1,0:T(8,128)(2,1)} %param.16, bf16[218,1024]{1,0:T(8,128)(2,1)} %collective-permute-done, s32[256]{0:T(256)S(1)} %bitcast.139, ...), kind=kOutput, calls=%fused_computation.200 | convolution fusion | flops 512426752 | bytes 3381248 | tf_op jit(solution)/shard_map/dot_general | solution.py:126
  451.5 4.9 convolution_convert_fusion
  457.5 3.9 collective-permute-start.3
  467.8 15.0 %collective-permute-done.3 = bf16[256,2048]{1,0:T(8,128)(2,1)} collective-permute-done((bf16[256,2048]{1,0:T(8,128)(2,1)}, bf16[256,2048]{1,0:T(8,128)(2,1)}, u32[]{:S(2)}, u32[]{:S(2)}) %collective-permute-start.3) | collective-permute-done | bytes 1048608 | tf_op jit(solution)/shard_map/ppermute | solution.py:23
  482.8 6.1 %collective-permute-done.2 = bf16[256,2048]{1,0:T(8,128)(2,1)} collective-permute-done((bf16[256,2048]{1,0:T(8,128)(2,1)}, bf16[256,2048]{1,0:T(8,128)(2,1)}, u32[]{:S(2)}, u32[]{:S(2)}) %collective-permute-start.2) | collective-permute-done | bytes 1048608 | tf_op jit(solution)/shard_map/ppermute | solution.py:20
  492.9 2.6 copy.60
  495.5 2.6 copy.62
  498.1 11.4 %fusion.128 = (f32[16,256]{1,0:T(8,128)S(1)}, f32[16,256,768]{2,1,0:T(8,128)}) fusion(pred[256,768]{1,0:T(8,128)(4,1)S(1)} %fusion.90, bf16[256,16,64]{0,2,1:T(8,128)(2,1)} %bitcast.124, bf16[768,16,64]{0,2,1:T(8,128)(2,1)} %bitcast.120), kind=kOutput, calls=%fused_computation.201 | convolution fusion | flops 418382592 | bytes 14893056 | tf_op jit(solution)/shard_map/sub | solution.py:86
  509.5 7.1 %fusion.77 = bf16[16,64,256]{2,1,0:T(8,128)(2,1)S(1)} fusion(bf16[768,16,64]{0,2,1:T(8,128)(2,1)} %bitcast.119, f32[16,256,768]{2,1,0:T(8,128)} %get-tuple-element.54, f32[16,256]{1,0:T(8,128)S(1)} %get-tuple-element.53), kind=kOutput, calls=%fused_computation.103 | convolution fusion | flops 409206784 | bytes 14696448 | tf_op jit(solution)/shard_map/hqk,khd->qhd/dot_general | solution.py:88
  518.8 7.7 %copy.64 = bf16[2,4,8,16,4096]{4,3,2,1,0:T(8,128)(2,1)} copy(bf16[2,4,8,16,4096]{4,3,0,1,2:T(8,128)(2,1)} %bitcast.111) | data formatting | bytes 16777216 | tf_op jit(solution)/shard_map/transpose | solution.py:44
  526.5 7.9 %copy.63 = bf16[2,4,8,16,4096]{4,3,2,1,0:T(8,128)(2,1)} copy(bf16[2,4,8,16,4096]{4,3,0,1,2:T(8,128)(2,1)} %bitcast.29) | data formatting | bytes 16777216 | tf_op jit(solution)/shard_map/transpose | solution.py:44
  534.4 12.1 %fusion.130 = (f32[256]{0:T(256)S(1)}, f32[256,1024]{1,0:T(8,128)}) fusion(f32[256,1024]{1,0:T(8,128)S(1)} %copy-done.2, bf16[1024,4096]{1,0:T(8,128)(2,1)} %bitcast.112, bf16[1024,4096]{1,0:T(8,128)(2,1)} %bitcast.113, f32[1024]{0:T(1024)S(1)} %bitcast.136, f32[256]{0:T(256)S(1)} %add_rsqrt_fusion.1, f32[256]{0:T(256)S(1)} %broadcast_multiply_fusion.1), kind=kOutput, calls=%fused_computation.203 | convolution fusion | flops 4305977344 | bytes 18881536 | tf_op jit(solution)/shard_map/dot_general | solution.py:63
  551.5 3.9 collective-permute-start.4
  557.2 4.5 collective-permute-done.4
  561.9 2.8 gather_fusion.3
  564.7 2.8 gather_fusion.2
  567.6 4.0 gather_fusion.1
  571.6 4.0 gather_fusion
  575.6 3.8 fusion.93
  579.4 3.9 all-to-all-start.6
  584.1 9.5 %all-to-all-done.6 = f32[1,100,1024]{1,0,2:T(1,128)S(1)} async-done(((f32[1,100,1024]{1,0,2:T(1,128)}), f32[1,100,1024]{1,0,2:T(1,128)S(1)}, u32[]{:S(2)}, u32[]{:S(2)}) %all-to-all-start.6) | async-done | bytes 409632 | tf_op jit(solution)/shard_map/all_to_all | solution.py:160
  594.3 9.4 %all_to_all.61 = bf16[4,100,256]{2,1,0:T(8,128)(2,1)S(1)} all-to-all(bf16[4,100,256]{2,1,0:T(8,128)(2,1)S(1)} %subtract_convert_fusion), channel_id=1, replica_groups=mesh['member'=4,'node_0'=2,'node_1'=4,'node_2'=8] {'member'}, dimensions={0} | all-to-all | bytes 409600 | tf_op jit(solution)/shard_map/all_to_all | solution.py:170
  (81 shorter events, 32.2 us)
Async XLA Ops:
  0.0 516.6 %copy-start = (bf16[1024,1024]{1,0:T(8,128)(2,1)S(1)}, bf16[1024,1024]{1,0:T(8,128)(2,1)}, u32[]{:S(2)}) copy-start(bf16[1024,1024]{1,0:T(8,128)(2,1)} %param.26) | copy-start | bytes 6291460
  1.8 8.8 %all-to-all-start.3 = ((bf16[2,1,16,4096]{3,2,1,0:T(8,128)(2,1)}), bf16[2,1,16,4096]{3,2,1,0:T(8,128)(2,1)S(1)}, u32[]{:S(2)}, u32[]{:S(2)}) async-start(bf16[2,1,16,4096]{3,2,1,0:T(8,128)(2,1)} %pad_maximum_fusion.2), calls=%async_computation.3 | async-start | bytes 524288 | tf_op jit(solution)/shard_map/all_to_all | solution.py:38
  244.6 5.2 copy-start.4
  244.6 14.1 %copy-start.10 = (s32[256]{0:T(256)S(1)}, s32[256]{0:T(256)}, u32[]{:S(2)}) copy-start(s32[256]{0:T(256)} %param.19) | copy-start | bytes 3076
  244.6 14.2 %copy-start.5 = (s32[1024,4]{0,1:T(4,128)S(1)}, s32[1024,4]{0,1:T(4,128)}, u32[]{:S(2)}) copy-start(s32[1024,4]{0,1:T(4,128)} %param.21) | copy-start | bytes 49156
  244.6 14.3 %copy-start.6 = (s32[256,16]{0,1:T(8,128)S(1)}, s32[256,16]{0,1:T(8,128)}, u32[]{:S(2)}) copy-start(s32[256,16]{0,1:T(8,128)} %param.18) | copy-start | bytes 49156
  244.6 14.3 %copy-start.7 = (f32[3,1024]{1,0:T(4,128)S(1)}, f32[3,1024]{1,0:T(4,128)}, u32[]{:S(2)}) copy-start(f32[3,1024]{1,0:T(4,128)} %param.24) | copy-start | bytes 36868
  244.6 281.9 %all-to-all-start.2 = ((bf16[8,8,16,4096]{3,2,1,0:T(8,128)(2,1)}), bf16[8,8,16,4096]{3,2,1,0:T(8,128)(2,1)}, u32[]{:S(2)}, u32[]{:S(2)}) async-start(bf16[8,8,16,4096]{3,2,1,0:T(8,128)(2,1)} %stack.20), calls=%async_computation.2 | async-start | bytes 16777216 | tf_op jit(solution)/shard_map/all_to_all | solution.py:38
  249.8 186.0 %collective-permute-start.1 = (bf16[218,1024]{1,0:T(8,128)(2,1)S(1)}, bf16[218,1024]{1,0:T(8,128)(2,1)S(1)}, u32[]{:S(2)}, u32[]{:S(2)}) collective-permute-start(bf16[218,1024]{1,0:T(8,128)(2,1)S(1)} %copy-done.4), channel_id=1, source_target_pairs={{1,0},{2,1},{3,2},{4,3},{5,4},{6,5},{7,6},{8,7},{9,8},{10,9},{11,1... | collective-permute-start | bytes 1339400 | tf_op jit(solution)/shard_map/ppermute | solution.py:23
  256.6 182.5 %collective-permute-start = (bf16[218,1024]{1,0:T(8,128)(2,1)S(1)}, bf16[218,1024]{1,0:T(8,128)(2,1)}, u32[]{:S(2)}, u32[]{:S(2)}) collective-permute-start(bf16[218,1024]{1,0:T(8,128)(2,1)S(1)} %copy-done.4), channel_id=1, source_target_pairs={{0,1},{1,2},{2,3},{3,4},{4,5},{5,6},{6,7},{7,8},{8,9},{9,10},{10,1... | collective-permute-start | bytes 1339400 | tf_op jit(solution)/shard_map/ppermute | solution.py:20
  435.8 3.3 copy-start.12
  451.5 13.1 %copy-start.11 = (s32[256]{0:T(256)S(1)}, s32[256]{0:T(256)}, u32[]{:S(2)}) copy-start(s32[256]{0:T(256)} %param.20) | copy-start | bytes 3076
  457.5 25.3 %collective-permute-start.3 = (bf16[256,2048]{1,0:T(8,128)(2,1)}, bf16[256,2048]{1,0:T(8,128)(2,1)}, u32[]{:S(2)}, u32[]{:S(2)}) collective-permute-start(bf16[256,2048]{1,0:T(8,128)(2,1)} %slice.157), channel_id=1, source_target_pairs={{1,0},{2,1},{3,2},{4,3},{5,4},{6,5},{7,6},{8,7},{9,8},{10,9},{11,1... | collective-permute-start | bytes 3145736 | tf_op jit(solution)/shard_map/ppermute | solution.py:23
  461.5 27.5 %collective-permute-start.2 = (bf16[256,2048]{1,0:T(8,128)(2,1)}, bf16[256,2048]{1,0:T(8,128)(2,1)}, u32[]{:S(2)}, u32[]{:S(2)}) collective-permute-start(bf16[256,2048]{1,0:T(8,128)(2,1)} %slice.157), channel_id=1, source_target_pairs={{0,1},{1,2},{2,3},{3,4},{4,5},{5,6},{6,7},{7,8},{8,9},{9,10},{10,1... | collective-permute-start | bytes 3145736 | tf_op jit(solution)/shard_map/ppermute | solution.py:20
  517.5 1.1 copy-start.1
  526.5 7.9 %copy-start.2 = (f32[256,1024]{1,0:T(8,128)S(1)}, f32[256,1024]{1,0:T(8,128)}, u32[]{:S(2)}) copy-start(f32[256,1024]{1,0:T(8,128)} %copy-done.1) | copy-start | bytes 3145732
  534.4 13.6 %copy-start.3 = (bf16[1024,100]{0,1:T(8,128)(2,1)S(1)}, bf16[1024,100]{0,1:T(8,128)(2,1)}, u32[]{:S(2)}) copy-start(bf16[1024,100]{0,1:T(8,128)(2,1)} %param.29) | copy-start | bytes 614404
  549.5 7.7 %collective-permute-start.5 = (bf16[100,256]{1,0:T(8,128)(2,1)S(1)}, bf16[100,256]{1,0:T(8,128)(2,1)S(1)}, u32[]{:S(2)}, u32[]{:S(2)}) collective-permute-start(bf16[100,256]{1,0:T(8,128)(2,1)S(1)} %fusion.80), channel_id=1, source_target_pairs={{1,0},{2,1},{3,2},{4,3},{5,4},{6,5},{7,6},{8,7},{9,8},{10,9},{11,1... | collective-permute-start | bytes 153608 | tf_op jit(solution)/shard_map/ppermute | solution.py:23
  551.5 10.2 %collective-permute-start.4 = (bf16[100,256]{1,0:T(8,128)(2,1)S(1)}, bf16[100,256]{1,0:T(8,128)(2,1)S(1)}, u32[]{:S(2)}, u32[]{:S(2)}) collective-permute-start(bf16[100,256]{1,0:T(8,128)(2,1)S(1)} %fusion.80), channel_id=1, source_target_pairs={{0,1},{1,2},{2,3},{3,4},{4,5},{5,6},{6,7},{7,8},{8,9},{9,10},{10,1... | collective-permute-start | bytes 153608 | tf_op jit(solution)/shard_map/ppermute | solution.py:20
  567.6 8.0 %copy-start.8 = (pred[1024]{0:T(1024)(128)(4,1)S(1)}, pred[1024]{0:T(1024)(128)(4,1)}, u32[]{:S(2)}) copy-start(pred[1024]{0:T(1024)(128)(4,1)} %get-tuple-element.62) | copy-start | bytes 3076
  571.6 4.0 copy-start.9
  579.4 14.2 %all-to-all-start.6 = ((f32[1,100,1024]{1,0,2:T(1,128)}), f32[1,100,1024]{1,0,2:T(1,128)S(1)}, u32[]{:S(2)}, u32[]{:S(2)}) async-start(f32[1,100,1024]{1,0,2:T(1,128)} %bitcast.118), calls=%async_computation.6 | async-start | bytes 1048576 | tf_op jit(solution)/shard_map/all_to_all | solution.py:160
